TPU v7x, 32 devices: a whole 2x2x4 slice. The times are simulated.
32 devices in a mesh: rows: 16 (over z, y, x), rep: 2 (over core).
Axes of the slice: x: 2, y: 2, z: 4, core: 2. Of those that a mesh axis runs over, the one named last changes fastest.
Arguments:
- node_feats: bfloat16 [32768, 128], P('rows'), may hold values from -6 to 6
- w_in: bfloat16 [128, 256], replicated, may hold values from -0.5 to 0.5
- w_out: bfloat16 [256, 172], replicated
- labels: int32 [32768], P(('rows', 'rep')), may hold values from 0 to 171
- hub_rows: int32 [16, 2, 64], P('rows', 'rep'), may hold values from 0 to 2047, as said below
- send_rows: int32 [16, 2, 128], P('rows', 'rep'), may hold values from -1 to 2047, as said below
- adj_hub: bfloat16 [32768, 2, 1024], P('rows', 'rep'), may hold values from -0.125 to 0.125
- adj_sparse: bfloat16 [32768, 2, 128], P('rows', 'rep'), may hold values from -0.375 to 0.375
Outputs:
- logits: bfloat16 [32768, 172], P(('rows', 'rep'))
- grad_in: float32 [128, 256], replicated
- grad_out: float32 [256, 172], replicated
Inputs may be any that keep to these rules, and one draw needn't show every extreme that they name: `hub_rows`: within each owner slab the 2 x 64 hub nodes are distinct. `send_rows`: for each source, half and destination the live slots (not -1) come first; their count is 1 to 8, and for every source and half some destination has all 8 slots live. A node may fill several slots.
All inputs are finite; a program needn't handle non-finite values.
Results may differ from a plain program's by a relative error of at most 0.0095.
The roundings to bfloat16 on the way count: a program that leaves them out, or rounds other values in their place, can miss the bound.
Values may be sent and summed in bfloat16 or wider, within the bound.
A program may use at most 128 MiB of HBM per device.

v0:
```python
import jax
import jax.numpy as jnp
from jax import lax
from jax.sharding import PartitionSpec as P

F32 = jnp.float32
BF16 = jnp.bfloat16


def dot(a, b, dims=((1,), (0,))):
    return lax.dot_general(a, b, (dims, ((), ())), preferred_element_type=F32)


def split_dot(a, b, dims=((1,), (0,)), split=0):
    wide = (a, b)[split]
    high = wide.astype(BF16)
    low = (wide - high.astype(F32)).astype(BF16)
    if split == 0:
        return dot(high, b, dims) + dot(low, b, dims)
    return dot(a, high, dims) + dot(a, low, dims)


def on_device(node_feats, w_in, w_out, labels, hub_rows, send_rows, adj_hub, adj_sparse):
    nrows = lax.axis_size("rows")
    slab = node_feats.shape[0]
    total_nodes = slab * nrows
    hubs = hub_rows.shape[2]
    cap = send_rows.shape[2] // nrows
    hub_mat = adj_hub[:, 0, :]
    sparse_mat = adj_sparse[:, 0, :]
    iota = jnp.arange(slab, dtype=jnp.int32)
    mine = jnp.concatenate([hub_rows[0, 0], send_rows[0, 0]])
    both = lax.all_gather(mine, "rep", axis=0, tiled=True)
    pick = (both[:, None] == iota[None, :]).astype(BF16)
    pick_mine = (mine[:, None] == iota[None, :]).astype(BF16)
    hub_sel = dot(pick, hub_mat).astype(BF16)
    sparse_sel = dot(pick, sparse_mat).astype(BF16)

    def spread(rows):
        panel = lax.all_gather(rows[:hubs], "rows", axis=0, tiled=True)
        got = lax.all_to_all(
            rows[hubs:].reshape(nrows, cap, -1), "rows", split_axis=0, concat_axis=0, tiled=True
        )
        return panel, got.reshape(nrows * cap, -1)

    panel, got = spread(dot(pick_mine, node_feats).astype(BF16))
    part = dot(hub_sel, panel) + dot(sparse_sel, got)
    first = lax.psum_scatter(part, "rep", scatter_dimension=0, tiled=True).astype(BF16)
    pre = dot(first, w_in)
    hidden = jnp.maximum(pre, 0.0).astype(BF16)
    panel, got = spread(hidden)
    part = dot(hub_mat, panel) + dot(sparse_mat, got)
    second = lax.psum_scatter(part, "rep", scatter_dimension=0, tiled=True).astype(BF16)
    scores = dot(second, w_out)
    classes = scores.shape[1]
    top = jnp.max(scores, axis=1, keepdims=True)
    expo = jnp.exp(scores - top)
    probs = expo / jnp.sum(expo, axis=1, keepdims=True)
    onehot = (labels[:, None] == jnp.arange(classes, dtype=jnp.int32)[None, :]).astype(F32)
    dscore = (probs - onehot) * (1.0 / jnp.sqrt(F32(total_nodes)))
    grad_out = split_dot(second, dscore, ((0,), (0,)), 1)
    full = lax.all_gather(dscore.astype(BF16), "rep", axis=0, tiled=True)
    hub_terms = dot(hub_mat, full, ((0,), (0,)))
    slot_terms = dot(sparse_mat, full, ((0,), (0,))).astype(BF16).reshape(nrows, cap, classes)
    hub_grad = lax.psum_scatter(hub_terms, "rows", scatter_dimension=0, tiled=True)
    returned = lax.all_to_all(slot_terms, "rows", split_axis=0, concat_axis=0, tiled=True)
    back = jnp.concatenate([hub_grad, returned.reshape(nrows * cap, classes).astype(F32)])
    dhidden = split_dot(back, w_out, ((1,), (1,)))
    dpre = jnp.where(pre > 0, dhidden, 0.0)
    grad_in = split_dot(first, dpre, ((0,), (0,)), 1)
    grad_in, grad_out = lax.psum((grad_in, grad_out), ("rows", "rep"))
    return scores.astype(BF16), grad_in, grad_out


def solution(mesh):
    return jax.shard_map(
        on_device,
        mesh=mesh,
        in_specs=(
            P("rows", None),
            P(),
            P(),
            P(("rows", "rep")),
            P("rows", "rep", None),
            P("rows", "rep", None),
            P("rows", "rep", None),
            P("rows", "rep", None),
        ),
        out_specs=(P(("rows", "rep"), None), P(), P()),
        check_vma=False,
    )
```

profile of v0, /device:TPU:0, one launch (start us, length us, event | category | flops | bytes accessed | tf_op | source)
XLA Modules:
  0.0 367.5 jit_solution(12745429699709212672)
XLA Ops:
  7.2 1.3 dynamic-slice
  9.1 0.8 fusion.51
  10.0 1.5 fusion.22
  12.1 8.3 %all-to-all-start = ((bf16[16,8,128]{2,1,0:T(8,128)(2,1)}), bf16[16,8,128]{2,1,0:T(8,128)(2,1)S(1)}, u32[]{:S(2)}, u32[]{:S(2)}) async-start(bf16[16,8,128]{2,1,0:T(8,128)(2,1)} %slice_bitcast_fusion.1), calls=%async_computation | async-start | bytes 65536 | tf_op jit(solution)/shard_map/all_to_all | solution.py:41
  20.5 1.8 all-reduce
  22.3 42.3 %all_gather.13 = bf16[1024,128]{1,0:T(8,128)(2,1)S(1)} all-gather(bf16[64,128]{1,0:T(8,128)(2,1)S(1)} %slice.16), channel_id=1, replica_groups=mesh['rows'=16,'rep'=2] {'rows'}, dimensions={0}, use_global_device_ids=true | all-gather | bytes 278528 | tf_op jit(solution)/shard_map/all_gather | solution.py:40
  64.7 4.4 %fusion.19 = f32[384,128]{1,0:T(8,128)S(1)} fusion(bf16[1024,128]{1,0:T(8,128)(2,1)S(1)} %all_gather.13, bf16[2048,1,1024]{2,0,1:T(8,128)(2,1)} %param.14, s32[384]{0:T(512)S(1)} %all-reduce), kind=kOutput, calls=%fused_computation.20 | convolution fusion | flops 1712455680 | bytes 4654592 | tf_op jit(solution)/shard_map/dot_general | solution.py:11
  69.1 1.5 convolution_add_fusion.1
  70.7 3.7 reduce-scatter.6.cloned.1.call-done
  74.4 1.7 maximum_convert_fusion
  76.1 0.6 slice_bitcast_fusion
  76.7 6.7 %all-to-all-start.1 = ((bf16[16,8,256]{2,1,0:T(8,128)(2,1)}), bf16[16,8,256]{2,1,0:T(8,128)(2,1)S(1)}, u32[]{:S(2)}, u32[]{:S(2)}) async-start(bf16[16,8,256]{2,1,0:T(8,128)(2,1)} %slice_bitcast_fusion), calls=%async_computation.2 | async-start | bytes 131072 | tf_op jit(solution)/shard_map/all_to_all | solution.py:41
  83.5 44.1 %all_gather.14 = bf16[1024,256]{1,0:T(8,128)(2,1)S(1)} all-gather(bf16[64,256]{1,0:T(8,128)(2,1)S(1)} %slice.18), channel_id=1, replica_groups=mesh['rows'=16,'rep'=2] {'rows'}, dimensions={0}, use_global_device_ids=true | all-gather | bytes 557056 | tf_op jit(solution)/shard_map/all_gather | solution.py:40
  127.6 3.5 fusion.2
  131.1 1.8 fusion.7
  133.0 5.6 %reduce-scatter.8.cloned.1.call-done = f32[1024,256]{0,1:T(8,128)} async-done(((f32[2048,256]{0,1:T(8,128)}), f32[1024,256]{0,1:T(8,128)}) %reduce-scatter.8.cloned.1.call-update) | async-done | bytes 1048592 | tf_op jit(solution)/shard_map/reduce_scatter | solution.py:53
  138.6 1.6 fusion.52
  140.4 1.0 fusion.33
  141.3 2.3 all_gather.15
  143.7 1.8 fusion.14
  145.5 2.5 copy.15
  148.4 0.7 copy.13
  149.1 6.9 %all-to-all-start.2 = ((bf16[16,8,172]{2,1,0:T(8,128)(2,1)}), bf16[16,8,172]{2,1,0:T(8,128)(2,1)S(1)}, u32[]{:S(2)}, u32[]{:S(2)}) async-start(bf16[16,8,172]{2,1,0:T(8,128)(2,1)} %bitcast.12), calls=%async_computation.4 | async-start | bytes 131072 | tf_op jit(solution)/shard_map/all_to_all | solution.py:66
  156.4 1.1 convolution_add_fusion.3
  157.6 6.1 %all-to-all-done.2 = bf16[16,8,172]{2,1,0:T(8,128)(2,1)S(1)} async-done(((bf16[16,8,172]{2,1,0:T(8,128)(2,1)}), bf16[16,8,172]{2,1,0:T(8,128)(2,1)S(1)}, u32[]{:S(2)}, u32[]{:S(2)}) %all-to-all-start.2) | async-done | bytes 44064 | tf_op jit(solution)/shard_map/all_to_all | solution.py:66
  163.7 64.5 %reduce-scatter.10.cloned.1.call-done = f32[64,172]{1,0:T(8,128)} async-done(((f32[1024,172]{1,0:T(8,128)}), f32[64,172]{1,0:T(8,128)}) %reduce-scatter.10.cloned.1.call-update) | async-done | bytes 44048 | tf_op jit(solution)/shard_map/reduce_scatter | solution.py:65
  228.1 1.0 fusion.31
  229.1 1.0 fusion.17
  230.4 0.9 convolution_add_fusion.4
  231.3 126.6 %all-reduce.4.cloned.1.call-done = (f32[128,256]{1,0:T(8,128)}, f32[256,172]{0,1:T(8,128)}) async-done(((f32[128,256]{1,0:T(8,128)}, f32[256,172]{0,1:T(8,128)}), (f32[128,256]{1,0:T(8,128)}, f32[256,172]{0,1:T(8,128)})) %all-reduce.4.cloned.1.call-update) | async-done | bytes 307216 | tf_op jit(solution)/shard_map/psum | solution.py:71
  357.8 1.6 copy.20
  359.4 1.6 copy.21
  (35 shorter events, 1.9 us)
Async XLA Ops:
  7.2 61.9 %copy-start = (bf16[2048,1,128]{2,0,1:T(8,128)(2,1)S(1)}, bf16[2048,1,128]{2,0,1:T(8,128)(2,1)}, u32[]{:S(2)}) copy-start(bf16[2048,1,128]{2,0,1:T(8,128)(2,1)} %param.15) | copy-start | bytes 1572868
  12.1 57.0 %all-to-all-start = ((bf16[16,8,128]{2,1,0:T(8,128)(2,1)}), bf16[16,8,128]{2,1,0:T(8,128)(2,1)S(1)}, u32[]{:S(2)}, u32[]{:S(2)}) async-start(bf16[16,8,128]{2,1,0:T(8,128)(2,1)} %slice_bitcast_fusion.1), calls=%async_computation | async-start | bytes 65536 | tf_op jit(solution)/shard_map/all_to_all | solution.py:41
  20.4 53.9 %reduce-scatter.6.cloned.1.call-start = ((), (), s32[]{:S(2)}) async-start(), calls=%async_computation.6 | async-start | bytes 294912 | tf_op jit(solution)/shard_map/reduce_scatter | solution.py:48
  64.7 9.7 %copy-start.6 = (bf16[128,256]{1,0:T(8,128)(2,1)S(1)}, bf16[128,256]{1,0:T(8,128)(2,1)}, u32[]{:S(2)}) copy-start(bf16[128,256]{1,0:T(8,128)(2,1)} %param.9) | copy-start | bytes 196612
  76.7 54.4 %all-to-all-start.1 = ((bf16[16,8,256]{2,1,0:T(8,128)(2,1)}), bf16[16,8,256]{2,1,0:T(8,128)(2,1)S(1)}, u32[]{:S(2)}, u32[]{:S(2)}) async-start(bf16[16,8,256]{2,1,0:T(8,128)(2,1)} %slice_bitcast_fusion), calls=%async_computation.2 | async-start | bytes 131072 | tf_op jit(solution)/shard_map/all_to_all | solution.py:41
  83.5 55.1 %reduce-scatter.8.cloned.1.call-start = ((), (), s32[]{:S(2)}) async-start(), calls=%async_computation.7 | async-start | bytes 3145728 | tf_op jit(solution)/shard_map/reduce_scatter | solution.py:53
  131.1 7.5 %copy-start.4 = (bf16[256,172]{0,1:T(8,128)(2,1)S(1)}, bf16[256,172]{0,1:T(8,128)(2,1)}, u32[]{:S(2)}) copy-start(bf16[256,172]{0,1:T(8,128)(2,1)} %param.10) | copy-start | bytes 264196
  132.9 7.5 %copy-start.7 = (s32[1024]{0:T(1024)S(1)}, s32[1024]{0:T(1024)}, u32[]{:S(2)}) copy-start(s32[1024]{0:T(1024)} %param.11) | copy-start | bytes 12292
  132.9 95.2 %reduce-scatter.10.cloned.1.call-start = ((), (), s32[]{:S(2)}) async-start(), calls=%async_computation.8 | async-start | bytes 1114112 | tf_op jit(solution)/shard_map/reduce_scatter | solution.py:65
  138.6 5.1 %copy-start.2 = (bf16[2048,1,1024]{2,0,1:T(8,128)(2,1)S(1)}, bf16[2048,1,1024]{2,0,1:T(8,128)(2,1)}, u32[]{:S(2)}) copy-start(bf16[2048,1,1024]{2,0,1:T(8,128)(2,1)} %param.14) | copy-start | bytes 12582916
  145.5 10.6 %copy-start.1 = (f32[1024,256]{0,1:T(8,128)S(1)}, f32[1024,256]{0,1:T(8,128)}, u32[]{:S(2)}) copy-start(f32[1024,256]{0,1:T(8,128)} %reduce-scatter.8.cloned.1.call-done) | copy-start | bytes 3145732
  149.1 14.5 %all-to-all-start.2 = ((bf16[16,8,172]{2,1,0:T(8,128)(2,1)}), bf16[16,8,172]{2,1,0:T(8,128)(2,1)S(1)}, u32[]{:S(2)}, u32[]{:S(2)}) async-start(bf16[16,8,172]{2,1,0:T(8,128)(2,1)} %bitcast.12), calls=%async_computation.4 | async-start | bytes 131072 | tf_op jit(solution)/shard_map/all_to_all | solution.py:66
  156.0 73.1 %copy-start.5 = (f32[192,256]{1,0:T(8,128)S(1)}, f32[192,256]{1,0:T(8,128)}, u32[]{:S(2)}) copy-start(f32[192,256]{1,0:T(8,128)} %get-tuple-element.10) | copy-start | bytes 589828
  156.0 201.8 %all-reduce.4.cloned.1.call-start = ((), (), s32[]{:S(2)}) async-start(), calls=%async_computation.9 | async-start | bytes 622592 | tf_op jit(solution)/shard_map/psum | solution.py:71
  156.4 73.7 %copy-start.3 = (f32[192,128]{1,0:T(8,128)S(1)}, f32[192,128]{1,0:T(8,128)}, u32[]{:S(2)}) copy-start(f32[192,128]{1,0:T(8,128)} %reduce-scatter.6.cloned.1.call-done) | copy-start | bytes 294916
Sparse Core Ops, SparseCore 0:
  70.8 3.5 reduce-scatter.5
  133.1 5.4 reduce-scatter.7
  148.2 79.9 reduce-scatter.9
  234.0 123.7 all-reduce.3
where the time goes:
time: 369 us; the launch traced here: 368 us
  waiting for transfers between devices  206 us (56%)
  blocking collectives  90.6 us (25%)
  matrix products  22.8 us (6%)
  starting transfers between devices  22.1 us (6%)
  between operations  14.6 us (4%)
  local copies, waits for them, and re-layouts  9.02 us (2%)
    psum x1, waiting for transfers between devices, on_device(): grad_in, grad_out = lax.psum((grad_in, grad_out), ('rows', 'rep'))  127 us
    all_gather x2, blocking collectives, spread(): panel = lax.all_gather(rows[:hubs], 'rows', axis=0, tiled=True)  86.4 us
    reduce_scatter x1, waiting for transfers between devices, on_device(): lax.psum_scatter(hub_terms, 'rows', scatter_dimension=0, tiled=True)  64.5 us
    dot_general x15, matrix products, dot(): return lax.dot_general(a, b, (dims, ((), ())), preferred_element_type=F32)  22.8 us
    all_to_all x2, starting transfers between devices, spread(): lax.all_to_all(rows[hubs:].reshape(nrows, cap, -1), 'rows', split_axis=0,...  15.1 us
    reduce_scatter x2, waiting for transfers between devices, on_device(): lax.psum_scatter(part, 'rep', scatter_dimension=0, tiled=True).astype(BF16)  9.28 us
  transfers between devices with their start and end apart: 7, of which 5 were waited for; matrix products, arithmetic and copies ran while one was open for 3% of the time, Pallas kernels for 0%

commit v1 on v0

v1 whole, which is shorter than its diff:
```python
import functools
import math

import jax
import jax.numpy as jnp
from jax import lax
from jax.experimental import pallas as pl
from jax.experimental.pallas import tpu as pltpu
from jax.sharding import PartitionSpec as P

F32 = jnp.float32
BF16 = jnp.bfloat16
MESH = pl.DeviceIdType.MESH


def dot(a, b):
    return lax.dot_general(a, b, (((1,), (0,)), ((), ())), preferred_element_type=F32)


def parts(wide):
    high = wide.astype(BF16)
    return high, (wide - high.astype(F32)).astype(BF16)


def kernel(
    n, hubs, cap, classes, block,
    feats, w_in, w_out, labels, entries, hub_hbm, sparse_hbm,
    logits, grad_in, grad_out,
    hub, sparse, others, sel_hub, sel_sparse,
    hub_out_x, slot_out_x, panel_x, got_x,
    part_out, part_in,
    hub_out_h, slot_out_h, panel_h, got_h,
    half_out, half_in, second, secondT, w_pad, w_padT, lab,
    ds, dsT, terms, slot_terms, hub_back, slot_back,
    go_out, go_in, go_mid, go_mid_in, gi_out, gi_in, gi_mid, gi_mid_in,
    load_sem, rep_send, rep_recv, row_send, row_recv,
):
    me = lax.axis_index("rows")
    h = lax.axis_index("rep")
    partner = 1 - h
    slab, feat = feats.shape
    half = slab // 2
    nblk = half // block
    count = entries.shape[0]
    wide = w_pad.shape[1]

    loads = [
        pltpu.make_async_copy(hub_hbm, hub, load_sem.at[0]),
        pltpu.make_async_copy(sparse_hbm, sparse, load_sem.at[1]),
    ]
    for load in loads:
        load.start()

    barrier = pltpu.get_barrier_semaphore()

    def greet(k, _):
        pl.semaphore_signal(
            barrier, inc=1, device_id={"rows": lax.rem(me + k, n)}, device_id_type=MESH
        )
        return 0

    lax.fori_loop(1, n, greet, 0)
    pl.semaphore_signal(barrier, inc=1, device_id={"rep": partner}, device_id_type=MESH)

    def to_partner(src, dst, i):
        return pltpu.make_async_remote_copy(
            src_ref=src, dst_ref=dst, send_sem=rep_send.at[i], recv_sem=rep_recv.at[i],
            device_id={"rep": partner}, device_id_type=MESH,
        )

    def to_row(src, dst, kind, k, slot, peer):
        return pltpu.make_async_remote_copy(
            src_ref=src, dst_ref=dst, send_sem=row_send.at[kind, k],
            recv_sem=row_recv.at[kind, slot], device_id={"rows": peer}, device_id_type=MESH,
        )

    def exchange_start(flows):
        def body(k, _):
            peer = lax.rem(me + k, n)
            for kind, src, dst in flows:
                to_row(src(peer), dst(me), kind, k, me, peer).start()
            return 0

        lax.fori_loop(1, n, body, 0)

    def exchange_wait(flows):
        def body(k, _):
            peer = lax.rem(me + n - k, n)
            for kind, src, dst in flows:
                to_row(src(peer), dst(peer), kind, k, peer, peer).wait_recv()
            return 0

        def sent(k, _):
            peer = lax.rem(me + k, n)
            for kind, src, dst in flows:
                to_row(src(peer), dst(me), kind, k, me, peer).wait_send()
            return 0

        lax.fori_loop(1, n, body, 0)
        lax.fori_loop(1, n, sent, 0)

    def rows_at(ref, size):
        return lambda i: ref.at[pl.ds(pl.multiple_of(i * size, size), size)]

    def spread_flows(kind, hub_out, slot_out, panel, got):
        return [
            (kind, lambda i: hub_out, rows_at(panel, hubs)),
            (kind + 1, rows_at(slot_out, cap), rows_at(got, cap)),
        ]

    def keep_own(hub_out, slot_out, panel, got):
        panel[pl.ds(pl.multiple_of(me * hubs, hubs), hubs), :] = hub_out[...]
        at = pl.ds(pl.multiple_of(me * cap, cap), cap)
        got[at, :] = slot_out[at, :]

    iota = lax.broadcasted_iota(jnp.int32, (count, slab), 1)
    pick = jnp.where(entries[:, :1] == iota, 1.0, 0.0).astype(BF16)
    chosen = dot(pick, feats[...])
    hub_out_x[...] = chosen[:hubs].astype(BF16)
    slot_out_x[...] = chosen[hubs:]
    keep_own(hub_out_x, slot_out_x, panel_x, got_x)
    w_pad[...] = jnp.zeros_like(w_pad)
    w_pad[:, :classes] = w_out[...]

    pl.semaphore_wait(barrier, n)
    swap_list = to_partner(entries, others, 0)
    swap_list.start()
    flows_x = spread_flows(0, hub_out_x, slot_out_x, panel_x, got_x)
    exchange_start(flows_x)

    w_padT[...] = jnp.transpose(w_pad[...].astype(F32)).astype(BF16)
    lab[...] = jnp.transpose(jnp.broadcast_to(labels[...].astype(F32), (128, half)))
    for load in loads:
        load.wait()
    swap_list.wait()
    picks = jnp.concatenate(
        [pick, jnp.where(others[:, :1] == iota, 1.0, 0.0).astype(BF16)], axis=0
    )
    step = 256

    def select(j, _):
        at = pl.ds(pl.multiple_of(j * step, step), step)
        sel_hub[:, at] = dot(picks, hub[:, at]).astype(BF16)
        return 0

    lax.fori_loop(0, n * hubs // step, select, 0)
    sel_sparse[...] = dot(picks, sparse[...]).astype(BF16)

    exchange_wait(flows_x)
    got = got_x[...].astype(BF16)
    part_out[...] = dot(sel_hub[count:, :], panel_x[...]) + dot(sel_sparse[count:, :], got)
    swap_part = to_partner(part_out, part_in, 1)
    swap_part.start()
    part = dot(sel_hub[:count, :], panel_x[...]) + dot(sel_sparse[:count, :], got)
    swap_part.wait()
    first32 = (part + part_in[...]).astype(BF16).astype(F32)
    pre = dot(first32.astype(BF16), w_in[...])
    hidden = jnp.maximum(pre, 0.0).astype(BF16)
    hub_out_h[...] = hidden[:hubs]
    slot_out_h[...] = hidden[hubs:].astype(F32)
    flows_h = spread_flows(2, hub_out_h, slot_out_h, panel_h, got_h)
    exchange_start(flows_h)
    keep_own(hub_out_h, slot_out_h, panel_h, got_h)
    firstT = jnp.transpose(first32).astype(BF16)
    exchange_wait(flows_h)

    got2 = got_h[...].astype(BF16)

    def partial_at(row):
        at = pl.ds(pl.multiple_of(row, block), block)
        return dot(hub[at, :], panel_h[...]) + dot(sparse[at, :], got2)

    def swap_half(i):
        at = pl.ds(pl.multiple_of(i * block, block), block)
        return to_partner(half_out.at[at], half_in.at[at], 2 + i)

    def give(i, _):
        at = pl.ds(pl.multiple_of(i * block, block), block)
        half_out[at, :] = partial_at(partner * half + i * block)
        swap_half(i).start()
        return 0

    lax.fori_loop(0, nblk, give, 0)

    scale = 1.0 / math.sqrt(slab * n)
    column = lax.broadcasted_iota(jnp.int32, (block, wide), 1)

    column_wide = column.astype(F32)

    def swap_ds(i):
        return to_partner(dsT.at[h, i], dsT.at[h, i], 2 + nblk + i)

    def score(i, _):
        at = pl.ds(pl.multiple_of(i * block, block), block)
        mine = partial_at(h * half + i * block)
        swap_half(i).wait()
        sec = (mine + half_in[at, :]).astype(BF16)
        second[at, :] = sec
        scores = dot(sec, w_pad[...])
        logits[at, :] = scores[:, :classes].astype(BF16)
        inside = column < classes
        top = jnp.max(jnp.where(inside, scores, -jnp.inf), axis=1, keepdims=True)
        expo = jnp.where(inside, jnp.exp(jnp.where(inside, scores - top, 0.0)), 0.0)
        probs = expo / jnp.sum(expo, axis=1, keepdims=True)
        hot = jnp.where(lab[at, :1] == column_wide, 1.0, 0.0)
        dscore = (probs - hot) * scale
        dsT[h, i, :, :] = jnp.transpose(dscore).astype(BF16)
        swap_ds(i).start()
        ds[at, :] = dscore
        secondT[:, at] = jnp.transpose(sec.astype(F32)).astype(BF16)
        return 0

    lax.fori_loop(0, nblk, score, 0)

    ds_high, ds_low = parts(ds[...])
    grad_out_part = dot(secondT[...], ds_high) + dot(secondT[...], ds_low)

    def fill(out, value):
        size = out.shape[1]
        for i in range(n):
            out[i] = value[i * size : (i + 1) * size]

    def reduce_flow(kind, out, into):
        return [(kind, lambda i: out.at[i], lambda i: into.at[i])]

    fill(go_out, grad_out_part)
    go_flow = reduce_flow(6, go_out, go_in)
    exchange_start(go_flow)

    def swap_ds_wait(i, _):
        swap_ds(i).wait_send()
        pltpu.make_async_remote_copy(
            src_ref=dsT.at[partner, i], dst_ref=dsT.at[partner, i],
            send_sem=rep_send.at[2 + nblk + i], recv_sem=rep_recv.at[2 + nblk + i],
            device_id={"rep": partner}, device_id_type=MESH,
        ).wait_recv()
        return 0

    lax.fori_loop(0, nblk, swap_ds_wait, 0)

    def gather_dsT():
        return jnp.concatenate([dsT[j, i] for j in range(2) for i in range(nblk)], axis=1)

    full = gather_dsT()
    tcols = 256

    def term(j, _):
        at = pl.ds(pl.multiple_of(j * tcols, tcols), tcols)
        terms[at, :] = jnp.transpose(dot(full, hub[:, at])).astype(BF16)
        return 0

    lax.fori_loop(0, n * hubs // tcols, term, 0)
    slot_terms[...] = jnp.transpose(dot(full, sparse[...]))
    back_flows = [
        (4, rows_at(terms, hubs), lambda i: hub_back.at[i]),
        (5, rows_at(slot_terms, cap), rows_at(slot_back, cap)),
    ]
    exchange_start(back_flows)
    hub_back[me] = terms[pl.ds(pl.multiple_of(me * hubs, hubs), hubs), :]
    own_slots = pl.ds(pl.multiple_of(me * cap, cap), cap)
    slot_back[own_slots, :] = slot_terms[own_slots, :]

    def total_of(into, out, mid, mid_in, i):
        into[me] = out[me]
        mid[...] = jnp.sum(into[...], axis=0)
        swap = to_partner(mid, mid_in, i)
        swap.start()
        swap.wait()
        return mid[...] + mid_in[...]

    def share(kind, grad):
        return [(kind, lambda i: grad.at[me], lambda i: grad.at[i])]

    exchange_wait(go_flow)
    grad_out[me] = total_of(go_in, go_out, go_mid, go_mid_in, 2 + 2 * nblk)
    go_share = share(7, grad_out)
    exchange_start(go_share)

    exchange_wait(back_flows)
    back = jnp.concatenate(
        [jnp.sum(hub_back[...].astype(F32), axis=0), slot_back[...]], axis=0
    )
    back_high, back_low = parts(back)
    dhidden = dot(back_high, w_padT[...]) + dot(back_low, w_padT[...])
    dpre_high, dpre_low = parts(jnp.where(pre > 0, dhidden, 0.0))
    fill(gi_out, dot(firstT, dpre_high) + dot(firstT, dpre_low))
    gi_flow = reduce_flow(8, gi_out, gi_in)
    exchange_start(gi_flow)
    exchange_wait(go_share)
    exchange_wait(gi_flow)
    grad_in[me] = total_of(gi_in, gi_out, gi_mid, gi_mid_in, 3 + 2 * nblk)
    gi_share = share(9, grad_in)
    exchange_start(gi_share)
    exchange_wait(gi_share)


def on_device(node_feats, w_in, w_out, labels, hub_rows, send_rows, adj_hub, adj_sparse):
    n = lax.axis_size("rows")
    slab, feat = node_feats.shape
    half = slab // lax.axis_size("rep")
    hid, classes = w_out.shape
    wide = -(-classes // 128) * 128
    hubs, slots = hub_rows.shape[2], send_rows.shape[2]
    cap = slots // n
    count = hubs + slots
    panel = n * hubs
    block = min(256, half)
    nblk = half // block
    mine = jnp.concatenate([hub_rows[0, 0], send_rows[0, 0]])
    entries = jnp.broadcast_to(mine[:, None], (count, 128))
    vmem = pltpu.VMEM
    scratch = [
        vmem((slab, panel), BF16), vmem((slab, slots), BF16), vmem((count, 128), jnp.int32),
        vmem((2 * count, panel), BF16), vmem((2 * count, slots), BF16),
        vmem((hubs, feat), BF16), vmem((slots, feat), F32), vmem((panel, feat), BF16), vmem((slots, feat), F32),
        vmem((count, feat), F32), vmem((count, feat), F32),
        vmem((hubs, hid), BF16), vmem((slots, hid), F32), vmem((panel, hid), BF16), vmem((slots, hid), F32),
        vmem((half, hid), F32), vmem((half, hid), F32), vmem((half, hid), BF16), vmem((hid, half), BF16),
        vmem((hid, wide), BF16), vmem((wide, hid), BF16), vmem((half, 128), F32),
        vmem((half, wide), F32), vmem((2, nblk, wide, block), BF16),
        vmem((panel, wide), BF16), vmem((slots, wide), F32),
        vmem((n, hubs, wide), BF16), vmem((slots, wide), F32),
        vmem((n, hid // n, wide), F32), vmem((n, hid // n, wide), F32),
        vmem((hid // n, wide), F32), vmem((hid // n, wide), F32),
        vmem((n, feat // n, hid), F32), vmem((n, feat // n, hid), F32),
        vmem((feat // n, hid), F32), vmem((feat // n, hid), F32),
        pltpu.SemaphoreType.DMA((2,)),
        pltpu.SemaphoreType.DMA((4 + 2 * nblk,)), pltpu.SemaphoreType.DMA((4 + 2 * nblk,)),
        pltpu.SemaphoreType.DMA((10, n)), pltpu.SemaphoreType.DMA((10, n)),
    ]
    in_vmem = pl.BlockSpec(memory_space=vmem)
    anywhere = pl.BlockSpec(memory_space=pl.ANY)
    logits, grad_in, grad_out = pl.pallas_call(
        functools.partial(kernel, n, hubs, cap, classes, block),
        out_shape=(
            jax.ShapeDtypeStruct((half, classes), BF16),
            jax.ShapeDtypeStruct((n, feat // n, hid), F32),
            jax.ShapeDtypeStruct((n, hid // n, wide), F32),
        ),
        in_specs=[in_vmem] * 5 + [anywhere] * 2,
        out_specs=(in_vmem,) * 3,
        scratch_shapes=scratch,
        compiler_params=pltpu.CompilerParams(
            collective_id=0, has_side_effects=True, vmem_limit_bytes=64_000_000
        ),
        name="gcn",
    )(
        node_feats, w_in, w_out, labels.reshape(1, half), entries,
        adj_hub[:, 0, :], adj_sparse[:, 0, :],
    )
    return logits, grad_in.reshape(feat, hid), grad_out.reshape(hid, wide)[:, :classes]


def solution(mesh):
    return jax.shard_map(
        on_device,
        mesh=mesh,
        in_specs=(
            P("rows", None),
            P(),
            P(),
            P(("rows", "rep")),
            P("rows", "rep", None),
            P("rows", "rep", None),
            P("rows", "rep", None),
            P("rows", "rep", None),
        ),
        out_specs=(P(("rows", "rep"), None), P(), P()),
        check_vma=False,
    )
```

time: 369 us -> 88.9 us (0.24)
  waiting for transfers between devices: 206 us -> 0 us
  blocking collectives: 90.6 us -> 0 us
  Pallas kernels: 0 us -> 79.6 us
  matrix products: 22.8 us -> 0 us
  starting transfers between devices: 22.1 us -> 0 us
  between operations: 14.6 us -> 0.64 us
    psum x1 -> x0, waiting for transfers between devices: 127 us -> none  [on_device(): grad_in, grad_out = lax.psum((grad_in, grad_out), ('rows', 'rep'))]
    all_gather x3 -> x0, blocking collectives: 88.7 us -> none  [the longest x2 86.4 us: spread(): panel = lax.all_gather(rows[:hubs], 'rows', axis=0, tiled=True)]
    pallas_call x0 -> x1, Pallas kernels: none -> 79.6 us  [on_device(): pl.pallas_call(functools.partial(kernel, n, hubs, cap, classes, block), o...]
    reduce_scatter x3 -> x0, waiting for transfers between devices: 73.8 us -> none  [the longest x1 64.5 us: on_device(): lax.psum_scatter(hub_terms, 'rows', scatter_dimension=0, tiled=True)]
    dot_general x15 -> x0, matrix products: 22.8 us -> none  [dot(): return lax.dot_general(a, b, (dims, ((), ())), preferred_element_type=F32)]
    all_to_all x3 -> x0, starting transfers between devices: 22 us -> none  [the longest x2 15.1 us: spread(): lax.all_to_all(rows[hubs:].reshape(nrows, cap, -1), 'rows', split_axis=0,...]
    all_to_all x3 -> x0, waiting for transfers between devices: 6.08 us -> none  [the longest x1 6.08 us: on_device(): lax.all_to_all(slot_terms, 'rows', split_axis=0, concat_axis=0, tiled=True)]
  transfers between devices with their start and end apart: 7 -> 0, of which waited for: 5 -> 0; matrix products, arithmetic and copies ran while one was open for 3% -> 0% of each run, Pallas kernels for 0% -> 0%
where the time goes in v1:
time: 88.9 us; the launch traced here: 88.6 us
  Pallas kernels  79.6 us (90%)
  local copies, waits for them, and re-layouts  7.65 us (9%)
    pallas_call x1, Pallas kernels, on_device(): pl.pallas_call(functools.partial(kernel, n, hubs, cap, classes, block), o...  79.6 us
    unnamed x4, local copies, waits for them, and re-layouts  6.91 us

profile of v1, /device:TPU:0, one launch (start us, length us, event | category | flops | bytes accessed | tf_op | source)
XLA Modules:
  0.0 88.6 jit_solution(4918903021775404622)
XLA Ops:
  0.6 0.7 pad_add_fusion
  1.4 0.7 broadcast_in_dim.2.entries
  2.1 1.6 %copy.11.w_out = bf16[256,172]{1,0:T(8,128)(2,1)} copy(bf16[256,172]{0,1:T(8,128)(2,1)} %param.10) | data formatting | bytes 176128 | tf_op args[2]
  3.8 79.6 %gcn.1 = (bf16[1024,172]{1,0:T(8,128)(2,1)}, f32[16,8,256]{2,1,0:T(8,128)}, f32[16,16,256]{2,1,0:T(8,128)}) custom-call(bf16[2048,128]{1,0:T(8,128)(2,1)} %feats.1, bf16[128,256]{1,0:T(8,128)(2,1)} %w_in.1, bf16[256,172]{1,0:T(8,128)(2,1)} %copy.11.w_out, s32[1,1024]{1,0:T(1,128)} %bitcast.12, s32[192,128]{1,0:T(8,128)} %broadcast_in_dim.2.entries, ...), custom_call_target="tpu_custom_call" | custom-call | tf_op jit(solution)/shard_map/gcn/pallas_call | solution.py:333
  83.4 2.0 %copy.13 = bf16[1024,172]{0,1:T(8,128)(2,1)} copy(bf16[1024,172]{1,0:T(8,128)(2,1)} %get-tuple-element.9) | data formatting | bytes 704512
  85.3 1.7 %copy.14 = f32[256,172]{0,1:T(8,128)} copy(f32[256,172]{1,0:T(8,128)} %bitcast.10) | data formatting | bytes 352256
  87.1 1.6 %copy.16 = f32[128,256]{1,0:T(8,128)} copy(f32[128,256]{1,0:T(8,128)} %bitcast.11) | data formatting | bytes 262144

commit v2 on v1

--- a/solution.py
+++ b/solution.py
@@ -24,16 +24,15 @@
 
 def kernel(
     n, hubs, cap, classes, block,
-    feats, w_in, w_out, labels, entries, hub_hbm, sparse_hbm,
+    feats, w_in, w_outT, labels, entries, hub_hbm, sparse_hbm,
     logits, grad_in, grad_out,
     hub, sparse, others, sel_hub, sel_sparse,
     hub_out_x, slot_out_x, panel_x, got_x,
     part_out, part_in,
     hub_out_h, slot_out_h, panel_h, got_h,
-    half_out, half_in, second, secondT, w_pad, w_padT, lab,
-    ds, dsT, terms, slot_terms, hub_back, slot_back,
-    go_out, go_in, go_mid, go_mid_in, gi_out, gi_in, gi_mid, gi_mid_in,
-    load_sem, rep_send, rep_recv, row_send, row_recv,
+    half_out, half_in, second, ds_low, dsT, terms, slot_terms, hub_back, slot_back,
+    go_out, go_in, go_mid, go_mid_in, go_all, gi_out, gi_in, gi_mid, gi_mid_in,
+    load_sem, rep_send, rep_recv, row_send, row_recv, z_send, z_recv, p_send, p_recv,
 ):
     me = lax.axis_index("rows")
     h = lax.axis_index("rep")
@@ -42,7 +41,9 @@
     half = slab // 2
     nblk = half // block
     count = entries.shape[0]
-    wide = w_pad.shape[1]
+    deep = z_send.shape[1]
+    plane = n // deep
+    my_z, my_p = me // plane, lax.rem(me, plane)
 
     loads = [
         pltpu.make_async_copy(hub_hbm, hub, load_sem.at[0]),
@@ -102,11 +103,72 @@
     def rows_at(ref, size):
         return lambda i: ref.at[pl.ds(pl.multiple_of(i * size, size), size)]
 
-    def spread_flows(kind, hub_out, slot_out, panel, got):
-        return [
-            (kind, lambda i: hub_out, rows_at(panel, hubs)),
-            (kind + 1, rows_at(slot_out, cap), rows_at(got, cap)),
-        ]
+    def z_copy(phase, src, panel, source, i, slot, peer):
+        return pltpu.make_async_remote_copy(
+            src_ref=src, dst_ref=rows_at(panel, hubs)(source), send_sem=z_send.at[phase, i],
+            recv_sem=z_recv.at[phase, slot], device_id={"rows": peer}, device_id_type=MESH,
+        )
+
+    def p_copy(phase, src, panel, source, i, k, z, slot, peer):
+        return pltpu.make_async_remote_copy(
+            src_ref=src, dst_ref=rows_at(panel, hubs)(source), send_sem=p_send.at[phase, i, k],
+            recv_sem=p_recv.at[phase, z, slot], device_id={"rows": peer}, device_id_type=MESH,
+        )
+
+    def pass_on(phase, src, panel, i, z, wait=False):
+        def body(k, _):
+            peer = my_z * plane + lax.rem(my_p + k, plane)
+            copy = p_copy(phase, src, panel, z * plane + my_p, i, k, z, my_p, peer)
+            copy.wait_send() if wait else copy.start()
+            return 0
+
+        lax.fori_loop(1, plane, body, 0)
+
+    def gather_start(phase, hub_out, panel):
+        def body(i, _):
+            peer = lax.rem(my_z + i, deep) * plane + my_p
+            z_copy(phase, hub_out, panel, me, i, my_z, peer).start()
+            return 0
+
+        lax.fori_loop(1, deep, body, 0)
+        pass_on(phase, hub_out, panel, 0, my_z)
+
+    def gather_wait(phase, hub_out, panel):
+        def arrive(i, _):
+            z = lax.rem(my_z + i, deep)
+            source = z * plane + my_p
+            z_copy(phase, hub_out, panel, source, i, z, source).wait_recv()
+            pass_on(phase, rows_at(panel, hubs)(source), panel, i, z)
+            return 0
+
+        lax.fori_loop(1, deep, arrive, 0)
+
+        def passed(i, _):
+            z = lax.rem(my_z + i, deep)
+
+            def body(k, _):
+                slot = lax.rem(my_p + k, plane)
+                p_copy(
+                    phase, hub_out, panel, z * plane + slot, i, k, z, slot, my_z * plane + slot
+                ).wait_recv()
+                return 0
+
+            lax.fori_loop(1, plane, body, 0)
+            return 0
+
+        lax.fori_loop(0, deep, passed, 0)
+
+        def sent(i, _):
+            peer = lax.rem(my_z + i, deep) * plane + my_p
+            z_copy(phase, hub_out, panel, me, i, my_z, peer).wait_send()
+            pass_on(phase, hub_out, panel, i, lax.rem(my_z + i, deep), True)
+            return 0
+
+        lax.fori_loop(1, deep, sent, 0)
+        pass_on(phase, hub_out, panel, 0, my_z, True)
+
+    def slot_flows(kind, slot_out, got):
+        return [(kind, rows_at(slot_out, cap), rows_at(got, cap))]
 
     def keep_own(hub_out, slot_out, panel, got):
         panel[pl.ds(pl.multiple_of(me * hubs, hubs), hubs), :] = hub_out[...]
@@ -119,17 +181,17 @@
     hub_out_x[...] = chosen[:hubs].astype(BF16)
     slot_out_x[...] = chosen[hubs:]
     keep_own(hub_out_x, slot_out_x, panel_x, got_x)
-    w_pad[...] = jnp.zeros_like(w_pad)
-    w_pad[:, :classes] = w_out[...]
+    terms[...] = jnp.zeros_like(terms)
+    slot_terms[...] = jnp.zeros_like(slot_terms)
+    go_out[...] = jnp.zeros_like(go_out)
 
     pl.semaphore_wait(barrier, n)
     swap_list = to_partner(entries, others, 0)
     swap_list.start()
-    flows_x = spread_flows(0, hub_out_x, slot_out_x, panel_x, got_x)
+    flows_x = slot_flows(1, slot_out_x, got_x)
+    gather_start(0, hub_out_x, panel_x)
     exchange_start(flows_x)
 
-    w_padT[...] = jnp.transpose(w_pad[...].astype(F32)).astype(BF16)
-    lab[...] = jnp.transpose(jnp.broadcast_to(labels[...].astype(F32), (128, half)))
     for load in loads:
         load.wait()
     swap_list.wait()
@@ -146,6 +208,7 @@
     lax.fori_loop(0, n * hubs // step, select, 0)
     sel_sparse[...] = dot(picks, sparse[...]).astype(BF16)
 
+    gather_wait(0, hub_out_x, panel_x)
     exchange_wait(flows_x)
     got = got_x[...].astype(BF16)
     part_out[...] = dot(sel_hub[count:, :], panel_x[...]) + dot(sel_sparse[count:, :], got)
@@ -158,10 +221,12 @@
     hidden = jnp.maximum(pre, 0.0).astype(BF16)
     hub_out_h[...] = hidden[:hubs]
     slot_out_h[...] = hidden[hubs:].astype(F32)
-    flows_h = spread_flows(2, hub_out_h, slot_out_h, panel_h, got_h)
+    flows_h = slot_flows(3, slot_out_h, got_h)
+    gather_start(1, hub_out_h, panel_h)
     exchange_start(flows_h)
     keep_own(hub_out_h, slot_out_h, panel_h, got_h)
     firstT = jnp.transpose(first32).astype(BF16)
+    gather_wait(1, hub_out_h, panel_h)
     exchange_wait(flows_h)
 
     got2 = got_h[...].astype(BF16)
@@ -183,9 +248,7 @@
     lax.fori_loop(0, nblk, give, 0)
 
     scale = 1.0 / math.sqrt(slab * n)
-    column = lax.broadcasted_iota(jnp.int32, (block, wide), 1)
-
-    column_wide = column.astype(F32)
+    class_of = lax.broadcasted_iota(jnp.int32, (classes, block), 0)
 
     def swap_ds(i):
         return to_partner(dsT.at[h, i], dsT.at[h, i], 2 + nblk + i)
@@ -196,29 +259,30 @@
         swap_half(i).wait()
         sec = (mine + half_in[at, :]).astype(BF16)
         second[at, :] = sec
-        scores = dot(sec, w_pad[...])
-        logits[at, :] = scores[:, :classes].astype(BF16)
-        inside = column < classes
-        top = jnp.max(jnp.where(inside, scores, -jnp.inf), axis=1, keepdims=True)
-        expo = jnp.where(inside, jnp.exp(jnp.where(inside, scores - top, 0.0)), 0.0)
-        probs = expo / jnp.sum(expo, axis=1, keepdims=True)
-        hot = jnp.where(lab[at, :1] == column_wide, 1.0, 0.0)
-        dscore = (probs - hot) * scale
-        dsT[h, i, :, :] = jnp.transpose(dscore).astype(BF16)
+        scores = lax.dot_general(
+            w_outT[...], sec, (((1,), (1,)), ((), ())), preferred_element_type=F32
+        )
+        logits[:, at] = scores.astype(BF16)
+        expo = jnp.exp(scores - jnp.max(scores, axis=0, keepdims=True))
+        probs = expo / jnp.sum(expo, axis=0, keepdims=True)
+        hot = jnp.where(labels[:, at] == class_of, 1.0, 0.0)
+        high, low = parts((probs - hot) * scale)
+        dsT[h, i, :, :] = high
         swap_ds(i).start()
-        ds[at, :] = dscore
-        secondT[:, at] = jnp.transpose(sec.astype(F32)).astype(BF16)
+        ds_low[:, at] = low
         return 0
 
     lax.fori_loop(0, nblk, score, 0)
 
-    ds_high, ds_low = parts(ds[...])
-    grad_out_part = dot(secondT[...], ds_high) + dot(secondT[...], ds_low)
+    ds_high = jnp.concatenate([dsT[h, i] for i in range(nblk)], axis=1)
+    grad_out_part = dot(ds_high, second[...]) + dot(ds_low[...], second[...])
 
     def fill(out, value):
         size = out.shape[1]
         for i in range(n):
-            out[i] = value[i * size : (i + 1) * size]
+            piece = value[i * size : (i + 1) * size]
+            if piece.shape[0]:
+                out[i, : piece.shape[0], :] = piece
 
     def reduce_flow(kind, out, into):
         return [(kind, lambda i: out.at[i], lambda i: into.at[i])]
@@ -246,11 +310,11 @@
 
     def term(j, _):
         at = pl.ds(pl.multiple_of(j * tcols, tcols), tcols)
-        terms[at, :] = jnp.transpose(dot(full, hub[:, at])).astype(BF16)
+        terms[at, :classes] = jnp.transpose(dot(full, hub[:, at])).astype(BF16)
         return 0
 
     lax.fori_loop(0, n * hubs // tcols, term, 0)
-    slot_terms[...] = jnp.transpose(dot(full, sparse[...]))
+    slot_terms[:, :classes] = jnp.transpose(dot(full, sparse[...]))
     back_flows = [
         (4, rows_at(terms, hubs), lambda i: hub_back.at[i]),
         (5, rows_at(slot_terms, cap), rows_at(slot_back, cap)),
@@ -272,16 +336,16 @@
         return [(kind, lambda i: grad.at[me], lambda i: grad.at[i])]
 
     exchange_wait(go_flow)
-    grad_out[me] = total_of(go_in, go_out, go_mid, go_mid_in, 2 + 2 * nblk)
-    go_share = share(7, grad_out)
+    go_all[me] = total_of(go_in, go_out, go_mid, go_mid_in, 2 + 2 * nblk)
+    go_share = share(7, go_all)
     exchange_start(go_share)
 
     exchange_wait(back_flows)
     back = jnp.concatenate(
         [jnp.sum(hub_back[...].astype(F32), axis=0), slot_back[...]], axis=0
     )
-    back_high, back_low = parts(back)
-    dhidden = dot(back_high, w_padT[...]) + dot(back_low, w_padT[...])
+    back_high, back_low = parts(back[:, :classes])
+    dhidden = dot(back_high, w_outT[...]) + dot(back_low, w_outT[...])
     dpre_high, dpre_low = parts(jnp.where(pre > 0, dhidden, 0.0))
     fill(gi_out, dot(firstT, dpre_high) + dot(firstT, dpre_low))
     gi_flow = reduce_flow(8, gi_out, gi_in)
@@ -291,6 +355,11 @@
     grad_in[me] = total_of(gi_in, gi_out, gi_mid, gi_mid_in, 3 + 2 * nblk)
     gi_share = share(9, grad_in)
     exchange_start(gi_share)
+    go_rows = go_all.shape[1]
+    for i in range(n):
+        size = min(go_rows, classes - i * go_rows)
+        if size > 0:
+            grad_out[pl.ds(i * go_rows, size), :] = go_all[i, :size, :]
     exchange_wait(gi_share)
 
 
@@ -305,6 +374,8 @@
     count = hubs + slots
     panel = n * hubs
     block = min(256, half)
+    piece = -(-classes // (8 * n)) * 8
+    deep = 4 if n % 4 == 0 else 1
     nblk = half // block
     mine = jnp.concatenate([hub_rows[0, 0], send_rows[0, 0]])
     entries = jnp.broadcast_to(mine[:, None], (count, 128))
@@ -315,27 +386,28 @@
         vmem((hubs, feat), BF16), vmem((slots, feat), F32), vmem((panel, feat), BF16), vmem((slots, feat), F32),
         vmem((count, feat), F32), vmem((count, feat), F32),
         vmem((hubs, hid), BF16), vmem((slots, hid), F32), vmem((panel, hid), BF16), vmem((slots, hid), F32),
-        vmem((half, hid), F32), vmem((half, hid), F32), vmem((half, hid), BF16), vmem((hid, half), BF16),
-        vmem((hid, wide), BF16), vmem((wide, hid), BF16), vmem((half, 128), F32),
-        vmem((half, wide), F32), vmem((2, nblk, wide, block), BF16),
+        vmem((half, hid), F32), vmem((half, hid), F32), vmem((half, hid), BF16),
+        vmem((classes, half), BF16), vmem((2, nblk, classes, block), BF16),
         vmem((panel, wide), BF16), vmem((slots, wide), F32),
         vmem((n, hubs, wide), BF16), vmem((slots, wide), F32),
-        vmem((n, hid // n, wide), F32), vmem((n, hid // n, wide), F32),
-        vmem((hid // n, wide), F32), vmem((hid // n, wide), F32),
+        vmem((n, piece, hid), F32), vmem((n, piece, hid), F32),
+        vmem((piece, hid), F32), vmem((piece, hid), F32), vmem((n, piece, hid), F32),
         vmem((n, feat // n, hid), F32), vmem((n, feat // n, hid), F32),
         vmem((feat // n, hid), F32), vmem((feat // n, hid), F32),
         pltpu.SemaphoreType.DMA((2,)),
         pltpu.SemaphoreType.DMA((4 + 2 * nblk,)), pltpu.SemaphoreType.DMA((4 + 2 * nblk,)),
         pltpu.SemaphoreType.DMA((10, n)), pltpu.SemaphoreType.DMA((10, n)),
+        pltpu.SemaphoreType.DMA((2, deep)), pltpu.SemaphoreType.DMA((2, deep)),
+        pltpu.SemaphoreType.DMA((2, deep, n // deep)), pltpu.SemaphoreType.DMA((2, deep, n // deep)),
     ]
     in_vmem = pl.BlockSpec(memory_space=vmem)
     anywhere = pl.BlockSpec(memory_space=pl.ANY)
     logits, grad_in, grad_out = pl.pallas_call(
         functools.partial(kernel, n, hubs, cap, classes, block),
         out_shape=(
-            jax.ShapeDtypeStruct((half, classes), BF16),
+            jax.ShapeDtypeStruct((classes, half), BF16),
             jax.ShapeDtypeStruct((n, feat // n, hid), F32),
-            jax.ShapeDtypeStruct((n, hid // n, wide), F32),
+            jax.ShapeDtypeStruct((classes, hid), F32),
         ),
         in_specs=[in_vmem] * 5 + [anywhere] * 2,
         out_specs=(in_vmem,) * 3,
@@ -345,10 +417,10 @@
         ),
         name="gcn",
     )(
-        node_feats, w_in, w_out, labels.reshape(1, half), entries,
+        node_feats, w_in, w_out.T, labels.reshape(1, half), entries,
         adj_hub[:, 0, :], adj_sparse[:, 0, :],
     )
-    return logits, grad_in.reshape(feat, hid), grad_out.reshape(hid, wide)[:, :classes]
+    return logits.T, grad_in.reshape(feat, hid), grad_out.T
 
 
 def solution(mesh):

time: 88.9 us -> 85.4 us (0.961)
  local copies, waits for them, and re-layouts: 7.65 us -> 5.65 us
  Pallas kernels: 79.6 us -> 78.1 us
    unnamed x4 -> x3, local copies, waits for them, and re-layouts: 6.91 us -> 4.91 us
    pallas_call x1, Pallas kernels: 79.6 us -> 78.1 us  [on_device(): pl.pallas_call(functools.partial(kernel, n, hubs, cap, classes, block), o...]
where the time goes in v2:
time: 85.4 us; the launch traced here: 85.1 us
  Pallas kernels  78.1 us (91%)
  local copies, waits for them, and re-layouts  5.65 us (7%)
    pallas_call x1, Pallas kernels, on_device(): pl.pallas_call(functools.partial(kernel, n, hubs, cap, classes, block), o...  78.1 us
    unnamed x3, local copies, waits for them, and re-layouts  4.91 us

profile of v2, /device:TPU:0, one launch (start us, length us, event | category | flops | bytes accessed | tf_op | source)
XLA Modules:
  0.0 85.1 jit_solution(10991998040953615517)
XLA Ops:
  0.6 0.7 pad_add_fusion
  1.4 0.7 broadcast_in_dim.2.entries
  2.1 78.1 %gcn.1 = (bf16[172,1024]{1,0:T(8,128)(2,1)}, f32[16,8,256]{2,1,0:T(8,128)}, f32[172,256]{1,0:T(8,128)}) custom-call(bf16[2048,128]{1,0:T(8,128)(2,1)} %feats.1, bf16[128,256]{1,0:T(8,128)(2,1)} %w_in.1, bf16[172,256]{1,0:T(8,128)(2,1)} %bitcast.14, s32[1,1024]{1,0:T(1,128)} %bitcast.15, s32[192,128]{1,0:T(8,128)} %broadcast_in_dim.2.entries, ...), custom_call_target="tpu_custom_call" | custom-call | tf_op jit(solution)/shard_map/gcn/pallas_call | solution.py:405
  80.2 1.7 %copy.14 = bf16[1024,172]{0,1:T(8,128)(2,1)} copy(bf16[1024,172]{0,1:T(8,128)(2,1)} %bitcast.11) | data formatting | bytes 704512
  82.0 1.6 %copy.15 = f32[128,256]{1,0:T(8,128)} copy(f32[128,256]{1,0:T(8,128)} %bitcast.13) | data formatting | bytes 262144
  83.5 1.6 %copy.16 = f32[256,172]{0,1:T(8,128)} copy(f32[256,172]{0,1:T(8,128)} %bitcast.12) | data formatting | bytes 352256
